TPU v7x, 32 devices: a whole 2x2x4 slice. The times are simulated.
32 devices in a mesh: replica: 4 (over y, x), shard: 8 (over z, core).
Axes of the slice: x: 2, y: 2, z: 4, core: 2. Of those that a mesh axis runs over, the one named last changes fastest.
Arguments:
- block_input: float32 [32, 224, 768], P(('replica', 'shard')), may hold values from -6 to 6
- out_cotangent: float32 [32, 224, 768], P(('replica', 'shard')), may hold values from -6 to 6
- ln1_gain: bfloat16 [768], P('shard'), may hold values from 0.5 to 1.5
- ln1_bias: bfloat16 [768], P('shard'), may hold values from -3 to 3
- attn_query: bfloat16 [768, 768], P('shard'), as said below
- query_bias: bfloat16 [768], P('shard'), may hold values from -3 to 3
- attn_key: bfloat16 [768, 768], P('shard'), may hold values from -0.21875 to 0.21875
- attn_value: bfloat16 [768, 768], P('shard'), may hold values from -0.21875 to 0.21875
- value_bias: bfloat16 [768], P('shard'), may hold values from -3 to 3
- attn_out: bfloat16 [768, 768], P('shard'), may hold values from -2 to 2
- out_bias: bfloat16 [768], P('shard'), may hold values from -3 to 3
- ln2_gain: bfloat16 [768], P('shard'), may hold values from 0.5 to 1.5
- ln2_bias: bfloat16 [768], P('shard'), may hold values from -3 to 3
- fc1_weight: bfloat16 [768, 3072], P('shard'), may hold values from -0.21875 to 0.21875
- fc1_bias: bfloat16 [3072], P('shard'), may hold values from -3 to 3
- fc2_weight: bfloat16 [3072, 768], P('shard'), may hold values from -0.21875 to 0.21875
- fc2_bias: bfloat16 [768], P('shard'), may hold values from -3 to 3
Outputs:
- block_output: float32 [32, 224, 768], P(('replica', 'shard'))
- input_grad: float32 [32, 224, 768], P(('replica', 'shard'))
- ln1_gain_grad: float32 [768], P('shard')
- ln1_bias_grad: float32 [768], P('shard')
- query_grad: float32 [768, 768], P('shard')
- query_bias_grad: float32 [768], P('shard')
- key_grad: float32 [768, 768], P('shard')
- value_grad: float32 [768, 768], P('shard')
- value_bias_grad: float32 [768], P('shard')
- out_grad: float32 [768, 768], P('shard')
- out_bias_grad: float32 [768], P('shard')
- ln2_gain_grad: float32 [768], P('shard')
- ln2_bias_grad: float32 [768], P('shard')
- fc1_grad: float32 [768, 3072], P('shard')
- fc1_bias_grad: float32 [3072], P('shard')
- fc2_grad: float32 [3072, 768], P('shard')
- fc2_bias_grad: float32 [768], P('shard')
Inputs may be any that keep to these rules, and one draw needn't show every extreme that they name: `attn_query`: weights of the query projection.
All inputs are finite; a program needn't handle non-finite values.
Results may differ from a plain program's by a relative error of at most 0.014.
The roundings to bfloat16 on the way count: a program that leaves them out, or rounds other values in their place, can miss the bound.
Values may be sent and summed in bfloat16 or wider, within the bound.
A program may use at most 128 MiB of HBM per device.

v0:
```python
import jax
import jax.numpy as jnp
from jax import lax
from jax.sharding import PartitionSpec as P

HEADS = 12
HEAD_DIM = 64


def matmul(spec, left, right):
    return jnp.einsum(spec, left, right, preferred_element_type=jnp.float32)


def normalize(inputs, gain, shift):
    center = inputs - jnp.mean(inputs, axis=-1, keepdims=True)
    inv_std = lax.rsqrt(jnp.mean(center * center, axis=-1, keepdims=True) + 1e-05)
    normed = center * inv_std
    act = (normed * gain.astype(jnp.float32) + shift.astype(jnp.float32)).astype(jnp.bfloat16)
    return (normed, inv_std, act)


def norm_back(grad_out, normed, inv_std, gain):
    scaled = grad_out * gain.astype(jnp.float32)
    return inv_std * (
        scaled
        - jnp.mean(scaled, axis=-1, keepdims=True)
        - normed * jnp.mean(scaled * normed, axis=-1, keepdims=True)
    )


def gelu_parts(pre):
    cdf = 0.5 * (1.0 + jax.scipy.special.erf(pre * 0.7071067811865476))
    dens = jnp.exp(-0.5 * pre * pre) * 0.3989422804014327
    return (pre * cdf, cdf + pre * dens)


def forward_pass(block_input, attn_full, mlp_full):
    ln1_gain, ln1_bias, attn_qkv, query_bias, value_bias, attn_out, out_bias = attn_full
    ln2_gain, ln2_bias, fc1_weight, fc1_bias, fc2_weight, fc2_bias = mlp_full
    f32 = jnp.float32
    bf16 = jnp.bfloat16
    clips, frames, width = block_input.shape
    scale = HEAD_DIM ** (-0.5)
    heads_shape = (clips, frames, HEADS, HEAD_DIM)
    normed1, inv1, act1 = normalize(block_input, ln1_gain, ln1_bias)
    mixed_in = matmul("cld,de->cle", act1, attn_qkv)
    query = ((mixed_in[..., :width] + query_bias.astype(f32)) * scale).astype(bf16)
    keys = mixed_in[..., width : 2 * width].astype(bf16)
    values = (mixed_in[..., 2 * width :] + value_bias.astype(f32)).astype(bf16)
    query, keys, values = (part.reshape(heads_shape) for part in (query, keys, values))
    scores = matmul("clhe,cmhe->chlm", query, keys)
    top = jnp.max(scores, axis=-1, keepdims=True)
    log_total = top + jnp.log(jnp.sum(jnp.exp(scores - top), axis=-1, keepdims=True))
    probs = jnp.exp(scores - log_total)
    mixed = (
        matmul("chlm,cmhe->clhe", probs.astype(bf16), values)
        .astype(bf16)
        .reshape(clips, frames, width)
    )
    middle = block_input + matmul("cld,de->cle", mixed, attn_out) + out_bias.astype(f32)
    normed2, inv2, act2 = normalize(middle, ln2_gain, ln2_bias)
    pre = matmul("cld,df->clf", act2, fc1_weight) + fc1_bias.astype(f32)
    activ, slope = gelu_parts(pre)
    activ_b = activ.astype(bf16)
    block_output = middle + matmul("clf,fd->cld", activ_b, fc2_weight) + fc2_bias.astype(f32)
    saved = (
        normed1,
        inv1,
        act1,
        query,
        keys,
        values,
        log_total,
        mixed,
        normed2,
        inv2,
        act2,
        slope,
        activ_b,
    )
    return (block_output, saved)


def backward_pass(out_cotangent, saved, attn_full, mlp_full):
    ln1_gain, ln1_bias, attn_qkv, query_bias, value_bias, attn_out, out_bias = attn_full
    ln2_gain, ln2_bias, fc1_weight, fc1_bias, fc2_weight, fc2_bias = mlp_full
    (
        normed1,
        inv1,
        act1,
        query,
        keys,
        values,
        log_total,
        mixed,
        normed2,
        inv2,
        act2,
        slope,
        activ_b,
    ) = saved
    bf16 = jnp.bfloat16
    clips, frames, width = out_cotangent.shape
    scale = HEAD_DIM ** (-0.5)
    heads_shape = (clips, frames, HEADS, HEAD_DIM)
    grad_b = out_cotangent.astype(bf16)
    fc2_grad = matmul("clf,cld->fd", activ_b, grad_b)
    fc2_bias_grad = jnp.sum(out_cotangent, axis=(0, 1))
    grad_pre = matmul("cld,fd->clf", grad_b, fc2_weight) * slope
    grad_pre_b = grad_pre.astype(bf16)
    fc1_grad = matmul("cld,clf->df", act2, grad_pre_b)
    fc1_bias_grad = jnp.sum(grad_pre, axis=(0, 1))
    grad_act2 = matmul("clf,df->cld", grad_pre_b, fc1_weight)
    ln2_gain_grad = jnp.sum(grad_act2 * normed2, axis=(0, 1))
    ln2_bias_grad = jnp.sum(grad_act2, axis=(0, 1))
    grad_middle = out_cotangent + norm_back(grad_act2, normed2, inv2, ln2_gain)
    grad_mid_b = grad_middle.astype(bf16)
    out_grad = matmul("cld,cle->de", mixed, grad_mid_b)
    out_bias_grad = jnp.sum(grad_middle, axis=(0, 1))
    grad_mixed = matmul("cle,de->cld", grad_mid_b, attn_out).astype(bf16).reshape(heads_shape)
    again = jnp.exp(matmul("clhe,cmhe->chlm", query, keys) - log_total)
    grad_probs = matmul("clhe,cmhe->chlm", grad_mixed, values)
    inner = jnp.sum(again * grad_probs, axis=-1, keepdims=True)
    grad_scores = (again * (grad_probs - inner)).astype(bf16)
    grad_query = matmul("chlm,cmhe->clhe", grad_scores, keys).reshape(clips, frames, width) * scale
    grad_keys = matmul("chlm,clhe->cmhe", grad_scores, query).reshape(clips, frames, width)
    grad_values = matmul("chlm,clhe->cmhe", again.astype(bf16), grad_mixed).reshape(
        clips, frames, width
    )
    query_bias_grad = jnp.sum(grad_query, axis=(0, 1))
    value_bias_grad = jnp.sum(grad_values, axis=(0, 1))
    grad_query_b = grad_query.astype(bf16)
    grad_keys_b = grad_keys.astype(bf16)
    grad_values_b = grad_values.astype(bf16)
    joined = jnp.concatenate((grad_query_b, grad_keys_b, grad_values_b), axis=-1)
    qkv_grad = matmul("cld,cle->de", act1, joined)
    grad_act1 = matmul("cle,de->cld", joined, attn_qkv)
    ln1_gain_grad = jnp.sum(grad_act1 * normed1, axis=(0, 1))
    ln1_bias_grad = jnp.sum(grad_act1, axis=(0, 1))
    input_grad = grad_middle + norm_back(grad_act1, normed1, inv1, ln1_gain)
    attn_grads = (
        ln1_gain_grad,
        ln1_bias_grad,
        qkv_grad,
        query_bias_grad,
        value_bias_grad,
        out_grad,
        out_bias_grad,
    )
    mlp_grads = (ln2_gain_grad, ln2_bias_grad, fc1_grad, fc1_bias_grad, fc2_grad, fc2_bias_grad)
    return (input_grad, attn_grads, mlp_grads)


def body(
    block_input,
    out_cotangent,
    ln1_gain,
    ln1_bias,
    attn_query,
    query_bias,
    attn_key,
    attn_value,
    value_bias,
    attn_out,
    out_bias,
    ln2_gain,
    ln2_bias,
    fc1_weight,
    fc1_bias,
    fc2_weight,
    fc2_bias,
):
    f32 = jnp.float32
    bf16 = jnp.bfloat16
    rows, width = attn_query.shape
    per_row = fc1_bias.shape[0] // rows
    narrow = (ln1_gain, ln1_bias, query_bias, value_bias, out_bias, ln2_gain, ln2_bias, fc2_bias)
    columns = jnp.concatenate((jnp.stack(narrow, axis=1), fc1_bias.reshape(rows, per_row)), axis=1)
    used = columns.shape[1]
    spare = -used % 128
    packed = jnp.concatenate(
        (attn_query, attn_key, attn_value, attn_out, jnp.pad(columns, ((0, 0), (0, spare)))), axis=1
    )
    attn_all = lax.all_gather(packed, "shard", axis=0, tiled=True)
    fc1_all = lax.all_gather(fc1_weight, "shard", axis=0, tiled=True)
    fc2_all = lax.all_gather(fc2_weight, "shard", axis=0, tiled=True)
    small = attn_all[:, 4 * width : 4 * width + used]
    g1, b1, bq, bv, bo, g2, b2, bf2 = (small[:, i] for i in range(len(narrow)))
    bf1 = small[:, len(narrow) :].reshape(-1)
    attn_full = (g1, b1, attn_all[:, : 3 * width], bq, bv, attn_all[:, 3 * width : 4 * width], bo)
    mlp_full = (g2, b2, fc1_all, bf1, fc2_all, bf2)
    block_output, saved = forward_pass(block_input, attn_full, mlp_full)
    input_grad, attn_grads, mlp_grads = backward_pass(out_cotangent, saved, attn_full, mlp_full)
    dg1, db1, dqkv, dbq, dbv, dout, dbo = attn_grads
    dg2, db2, dfc1, dbf1, dfc2, dbf2 = mlp_grads

    def owned(grad):
        part = lax.psum_scatter(grad.astype(bf16), "shard", scatter_dimension=0, tiled=True)
        return lax.psum(part, "replica").astype(f32)

    fc2_owned = owned(dfc2)
    fc1_owned = owned(dfc1)
    thin = jnp.concatenate(
        (jnp.stack((dg1, db1, dbq, dbv, dbo, dg2, db2, dbf2), axis=1), dbf1.reshape(-1, per_row)),
        axis=1,
    )
    attn_owned = owned(jnp.concatenate((dqkv, dout, jnp.pad(thin, ((0, 0), (0, spare)))), axis=1))
    base = 4 * width
    og1, ob1, obq, obv, obo, og2, ob2, obf2 = (attn_owned[:, base + i] for i in range(len(narrow)))
    obf1 = attn_owned[:, base + len(narrow) : base + used].reshape(-1)
    return (
        block_output,
        input_grad,
        og1,
        ob1,
        attn_owned[:, :width],
        obq,
        attn_owned[:, width : 2 * width],
        attn_owned[:, 2 * width : 3 * width],
        obv,
        attn_owned[:, 3 * width : 4 * width],
        obo,
        og2,
        ob2,
        fc1_owned,
        obf1,
        fc2_owned,
        obf2,
    )


def solution(mesh):
    placed = (
        P(("replica", "shard"), None, None),
        P(("replica", "shard"), None, None),
        P("shard"),
        P("shard"),
        P("shard", None),
        P("shard"),
        P("shard", None),
        P("shard", None),
        P("shard"),
        P("shard", None),
        P("shard"),
        P("shard"),
        P("shard"),
        P("shard", None),
        P("shard"),
        P("shard", None),
        P("shard"),
    )
    return jax.shard_map(
        body,
        mesh=mesh,
        in_specs=placed,
        out_specs=(
            P(("replica", "shard"), None, None),
            P(("replica", "shard"), None, None),
            P("shard"),
            P("shard"),
            P("shard", None),
            P("shard"),
            P("shard", None),
            P("shard", None),
            P("shard"),
            P("shard", None),
            P("shard"),
            P("shard"),
            P("shard"),
            P("shard", None),
            P("shard"),
            P("shard", None),
            P("shard"),
        ),
        check_vma=False,
    )
```

profile of v0, /device:TPU:0, one launch (start us, length us, event | category | flops | bytes accessed | tf_op | source)
XLA Modules:
  0.0 430.5 jit_solution(5986682349822183564)
XLA Ops:
  7.2 0.9 reshape.409
  9.1 0.9 constant_dynamic-update-slice_fusion.3
  10.1 0.9 constant_dynamic-update-slice_fusion.2
  11.0 0.9 constant_dynamic-update-slice_fusion.1
  11.9 0.9 constant_dynamic-update-slice_fusion
  15.6 54.1 %all-gather.4.cloned.1.call-done = bf16[768,3200]{1,0:T(8,128)(2,1)} async-done(((bf16[96,3200]{1,0:T(8,128)(2,1)}), bf16[768,3200]{1,0:T(8,128)(2,1)}) %all-gather.4.cloned.1.call-update) | async-done | bytes 4915216 | tf_op jit(solution)/shard_map/all_gather | solution.py:184
  69.7 1.0 slice_convert_fusion.1
  71.0 3.1 convert_reduce_fusion
  74.1 3.0 convolution_bitcast_fusion
  77.3 0.9 copy.96
  78.2 0.9 copy.97
  79.3 1.8 fusion.55
  82.3 1.9 fusion.56
  84.4 36.8 %all-gather.6.cloned.1.call-done = bf16[768,3072]{1,0:T(8,128)(2,1)} async-done(((bf16[96,3072]{1,0:T(8,128)(2,1)}), bf16[768,3072]{1,0:T(8,128)(2,1)}) %all-gather.6.cloned.1.call-update) | async-done | bytes 4718608 | tf_op jit(solution)/shard_map/all_gather | solution.py:185
  121.2 5.9 %multiply_convert_fusion.1 = (bf16[224,3072]{1,0:T(8,128)(2,1)}, f32[224,3072]{1,0:T(8,128)}) fusion(f32[3072]{0:T(1024)S(1)} %reshape.429, bf16[768,3072]{1,0:T(8,128)(2,1)} %all-gather.6.cloned.1.call-done, f32[1,224,768]{2,1,0:T(8,128)S(1)} %get-tuple-element.60, f32[768]{0:T(1024)S(1)} %get-tuple-element.18, f32[768]{0:T(1024)S(1)} %get-tuple-element.19, ...), kind=kOutput, calls=%fused_computation.19 | convolution fusion | flops 1061953536 | bytes 9555712 | tf_op jit(solution)/shard_map/cld,df->clf/dot_general | solution.py:11
  127.2 45.7 %all-gather.8.cloned.1.call-done = bf16[3072,768]{1,0:T(8,128)(2,1)} async-done(((bf16[384,768]{1,0:T(8,128)(2,1)}), bf16[3072,768]{1,0:T(8,128)(2,1)}) %all-gather.8.cloned.1.call-update) | async-done | bytes 4718608 | tf_op jit(solution)/shard_map/all_gather | solution.py:186
  172.9 5.2 %fusion.57 = (bf16[3072]{0:T(1024)(128)(2,1)S(1)}, bf16[224,3072]{1,0:T(8,128)(2,1)S(1)}) fusion(f32[224,3072]{1,0:T(8,128)} %get-tuple-element.62, bf16[3072,768]{1,0:T(8,128)(2,1)} %all-gather.8.cloned.1.call-done, f32[1,224,768]{2,1,0:T(8,128)} %param.18), kind=kOutput, calls=%fused_computation.121 | convolution fusion | flops 1064702976 | bytes 9541632 | tf_op jit(solution)/shard_map/cld,fd->clf/dot_general | solution.py:11
  178.2 1.2 copy-done.14
  179.3 3.8 convolution_convert_fusion.2
  183.2 5.1 %convolution_convert_fusion.1 = bf16[3072,768]{1,0:T(8,128)(2,1)} fusion(bf16[224,3072]{1,0:T(8,128)(2,1)} %get-tuple-element.61, f32[1,224,768]{2,1,0:T(8,128)} %param.18), kind=kOutput, calls=%fused_computation.3 | convolution fusion | flops 1059495936 | bytes 6782976 | tf_op jit(solution)/shard_map/clf,cld->fd/dot_general | solution.py:11
  188.5 1.1 reshape.420
  189.6 4.5 %fusion.19 = (bf16[768]{0:T(1024)(128)(2,1)S(1)}, f32[224]{0:T(256)S(1)}, f32[224,768]{1,0:T(8,128)S(1)}) fusion(f32[1,224,768]{2,1,0:T(8,128)S(1)} %get-tuple-element.60, f32[224]{0:T(256)S(1)} %add_rsqrt_fusion, f32[224]{0:T(256)S(1)} %broadcast_multiply_fusion.4, f32[768]{0:T(1024)S(1)} %get-tuple-element.19, ...), kind=kOutput, calls=%fused_computation.46 | convolution fusion | flops 1058167808 | bytes 7478400 | tf_op jit(solution)/shard_map/clf,df->cld/dot_general | solution.py:11
  194.7 0.9 stack.76
  195.5 0.9 stack.78
  196.4 0.9 stack.77
  198.1 2.6 convolution_convert_fusion.6
  200.7 1.9 copy.99
  202.6 2.4 fusion.52
  204.9 1.1 stack.75
  206.0 1.9 multiply_reduce_fusion
  208.5 1.1 copy-done
  210.0 1.1 stack.74
  211.1 2.0 convolution_convert_fusion.4
  213.2 3.7 fusion.20
  219.7 2.3 concatenate.20
  222.5 2.6 convolution_convert_fusion
  225.1 2.6 fusion.1
  227.8 9.1 %reduce-scatter.6.cloned.1.call-done = bf16[96,3072]{1,0:T(8,128)(2,1)} async-done(((bf16[768,3072]{1,0:T(8,128)(2,1)}), bf16[96,3072]{1,0:T(8,128)(2,1)}) %reduce-scatter.6.cloned.1.call-update) | async-done | bytes 589840 | tf_op jit(solution)/shard_map/reduce_scatter | solution.py:198
  236.9 55.5 %reduce-scatter.8.cloned.1.call-done = bf16[384,768]{1,0:T(8,128)(2,1)} async-done(((bf16[3072,768]{1,0:T(8,128)(2,1)}), bf16[384,768]{1,0:T(8,128)(2,1)}) %reduce-scatter.8.cloned.1.call-update) | async-done | bytes 589840 | tf_op jit(solution)/shard_map/reduce_scatter | solution.py:198
  292.5 57.4 %reduce-scatter.4.cloned.1.call-done = bf16[96,3200]{1,0:T(8,128)(2,1)} async-done(((bf16[768,3200]{1,0:T(8,128)(2,1)}), bf16[96,3200]{1,0:T(8,128)(2,1)}) %reduce-scatter.4.cloned.1.call-update) | async-done | bytes 614416 | tf_op jit(solution)/shard_map/reduce_scatter | solution.py:198
  349.9 2.2 fusion.23
  352.1 4.4 %fusion.13 = f32[1,224,768]{2,1,0:T(8,128)} fusion(f32[1,224,768]{2,1,0:T(8,128)S(1)} %get-tuple-element.60, bf16[224,3072]{1,0:T(8,128)(2,1)S(1)} %copy-done.11, bf16[3072,768]{1,0:T(8,128)(2,1)} %all-gather.8.cloned.1.call-done, f32[768]{0:T(1024)S(1)} %get-tuple-element.17), kind=kOutput, calls=%fused_computation.34 | convolution fusion | flops 1057308672 | bytes 7474176 | tf_op jit(solution)/shard_map/clf,fd->cld/dot_general | solution.py:11
  356.5 60.1 %all-reduce.5.cloned.1.call-done = (bf16[96,3200]{1,0:T(8,128)(2,1)}, bf16[96,3072]{1,0:T(8,128)(2,1)}, bf16[384,768]{1,0:T(8,128)(2,1)}) async-done(((bf16[96,3200]{1,0:T(8,128)(2,1)}, bf16[96,3072]{1,0:T(8,128)(2,1)}, bf16[384,768]{1,0:T(8,128)(2,1)}), (bf16[96,3200]{1,0:T(8,128)(2,1)}, bf16[96,3072]{1,0:T(8,128)(2,1)}, bf16[384,768]{1,0:T(8,128)(2,1)})) %all-reduce.5.cloned.1.call-update) | async-done | bytes 1794064 | tf_op jit(solution)/shard_map/psum | solution.py:199
  416.7 0.9 slice.144
  417.6 2.2 fusion.54
  420.6 1.1 convert_element_type.259
  421.7 1.1 convert_element_type.261
  422.8 0.9 slice_reduce_fusion
  (98 shorter events, 12.3 us)
Async XLA Ops:
  7.2 8.1 %copy-start.1 = (f32[1,224,768]{2,1,0:T(8,128)S(1)}, f32[1,224,768]{2,1,0:T(8,128)}, u32[]{:S(2)}) copy-start(f32[1,224,768]{2,1,0:T(8,128)} %param.17) | copy-start | bytes 2064388
  7.2 62.5 %all-gather.4.cloned.1.call-start = ((), (), s32[]{:S(2)}) async-start(), calls=%async_computation.3 | async-start | bytes 5529600 | tf_op jit(solution)/shard_map/all_gather | solution.py:184
  12.9 0.8 copy-start.15
  13.7 107.5 %all-gather.6.cloned.1.call-start = ((), (), s32[]{:S(2)}) async-start(), calls=%async_computation.4 | async-start | bytes 5308416 | tf_op jit(solution)/shard_map/all_gather | solution.py:185
  14.5 158.4 %all-gather.8.cloned.1.call-start = ((), (), s32[]{:S(2)}) async-start(), calls=%async_computation.5 | async-start | bytes 5308416 | tf_op jit(solution)/shard_map/all_gather | solution.py:186
  15.2 221.7 %reduce-scatter.6.cloned.1.call-start = ((), (), s32[]{:S(2)}) async-start(), calls=%async_computation.7 | async-start | bytes 5308416 | tf_op jit(solution)/shard_map/reduce_scatter | solution.py:198
  79.3 2.3 copy-start.7
  81.2 1.1 copy-start.2
  82.2 2.0 copy-start.9
  178.1 1.2 copy-start.14
  183.1 109.3 %reduce-scatter.8.cloned.1.call-start = ((), (), s32[]{:S(2)}) async-start(), calls=%async_computation.8 | async-start | bytes 5308416 | tf_op jit(solution)/shard_map/reduce_scatter | solution.py:198
  188.3 161.6 %reduce-scatter.4.cloned.1.call-start = ((), (), s32[]{:S(2)}) async-start(), calls=%async_computation.6 | async-start | bytes 5529600 | tf_op jit(solution)/shard_map/reduce_scatter | solution.py:198
  189.6 4.7 %copy-start.13 = (f32[1,224,768]{2,1,0:T(8,128)S(1)}, f32[1,224,768]{2,1,0:T(8,128)}, u32[]{:S(2)}) copy-start(f32[1,224,768]{2,1,0:T(8,128)} %param.18) | copy-start | bytes 2064388
  194.6 3.5 copy-start.4
  207.9 1.7 copy-start.8
  208.5 1.1 copy-start
  209.6 3.6 copy-start.3
  209.6 3.6 copy-start.24
  210.0 3.1 copy-start.25
  213.2 3.8 copy-start.26
  213.2 6.5 %copy-start.16 = (bf16[768,4]{1,0:T(8,128)(2,1)S(1)}, bf16[768,4]{1,0:T(8,128)(2,1)}, u32[]{:S(2)}) copy-start(bf16[768,4]{1,0:T(8,128)(2,1)} %reshape.420) | copy-start | bytes 18436
  213.2 6.5 %copy-start.17 = (bf16[768,1]{1,0:T(8,128)(2,1)S(1)}, bf16[768,1]{1,0:T(8,128)(2,1)}, u32[]{:S(2)}) copy-start(bf16[768,1]{1,0:T(8,128)(2,1)} %stack.76) | copy-start | bytes 4612
  213.2 6.4 %copy-start.18 = (bf16[768,1]{1,0:T(8,128)(2,1)S(1)}, bf16[768,1]{1,0:T(8,128)(2,1)}, u32[]{:S(2)}) copy-start(bf16[768,1]{1,0:T(8,128)(2,1)} %stack.78) | copy-start | bytes 4612
  213.2 6.4 %copy-start.19 = (bf16[768,1]{1,0:T(8,128)(2,1)S(1)}, bf16[768,1]{1,0:T(8,128)(2,1)}, u32[]{:S(2)}) copy-start(bf16[768,1]{1,0:T(8,128)(2,1)} %stack.77) | copy-start | bytes 4612
  213.2 6.4 %copy-start.20 = (bf16[768,1]{1,0:T(8,128)(2,1)S(1)}, bf16[768,1]{1,0:T(8,128)(2,1)}, u32[]{:S(2)}) copy-start(bf16[768,1]{1,0:T(8,128)(2,1)} %stack.79) | copy-start | bytes 4612
  217.0 0.8 copy-start.12
  217.0 5.0 %copy-start.5 = (f32[1,224,768]{2,1,0:T(8,128)S(1)}, f32[1,224,768]{2,1,0:T(8,128)}, u32[]{:S(2)}) copy-start(f32[1,224,768]{2,1,0:T(8,128)} %copy-done.4) | copy-start | bytes 2064388
  217.0 5.0 %copy-start.10 = (bf16[12,64,224]{2,1,0:T(8,128)(2,1)S(1)}, bf16[12,64,224]{2,1,0:T(8,128)(2,1)}, u32[]{:S(2)}) copy-start(bf16[12,64,224]{2,1,0:T(8,128)(2,1)} %copy-done.9) | copy-start | bytes 1032196
  222.5 2.6 copy-start.21
  227.7 124.4 %copy-start.11 = (bf16[224,3072]{1,0:T(8,128)(2,1)S(1)}, bf16[224,3072]{1,0:T(8,128)(2,1)}, u32[]{:S(2)}) copy-start(bf16[224,3072]{1,0:T(8,128)(2,1)} %get-tuple-element.61) | copy-start | bytes 4128772
  227.7 188.9 %all-reduce.5.cloned.1.call-start = ((), (), s32[]{:S(2)}) async-start(), calls=%async_computation.9 | async-start | bytes 3588096 | tf_op jit(solution)/shard_map/psum | solution.py:199
  416.7 3.1 copy-start.6
  416.7 3.9 copy-start.23
  417.6 4.1 copy-start.22
Sparse Core Ops, SparseCore 0:
  13.8 55.8 all-gather.3
  71.4 49.8 all-gather.5
  122.9 49.9 all-gather.7
  183.3 53.6 reduce-scatter.5
  239.1 53.3 reduce-scatter.7
  294.6 55.1 reduce-scatter.3
  353.4 63.2 all-reduce.4
where the time goes:
time: 431 us; the launch traced here: 430 us
  waiting for transfers between devices  320 us (74%)
  matrix products  52.4 us (12%)
  local copies, waits for them, and re-layouts  29.2 us (7%)
  between operations  14.6 us (3%)
  other arithmetic  13.6 us (3%)
    reduce_scatter x3, waiting for transfers between devices, owned(): lax.psum_scatter(grad.astype(bf16), 'shard', scatter_dimension=0, tiled=T...  122 us
    psum x1, waiting for transfers between devices, owned(): return lax.psum(part, 'replica').astype(f32)  60.1 us
    all_gather x1, waiting for transfers between devices, body(): attn_all = lax.all_gather(packed, 'shard', axis=0, tiled=True)  54.1 us
    dot_general x18, matrix products, matmul(): return jnp.einsum(spec, left, right, preferred_element_type=jnp.float32)  52.4 us
    all_gather x1, waiting for transfers between devices, body(): fc2_all = lax.all_gather(fc2_weight, 'shard', axis=0, tiled=True)  45.7 us
    all_gather x1, waiting for transfers between devices, body(): fc1_all = lax.all_gather(fc1_weight, 'shard', axis=0, tiled=True)  36.8 us
  transfers between devices with their start and end apart: 7, of which 7 were waited for; matrix products, arithmetic and copies ran while one was open for 16% of the time, Pallas kernels for 0%

commit v1 on v0

--- a/solution.py
+++ b/solution.py
@@ -5,6 +5,28 @@
 
 HEADS = 12
 HEAD_DIM = 64
+
+
+def joined_along(pieces, dim):
+    dims = list(pieces.shape[1:])
+    dims[dim] *= pieces.shape[0]
+    return jnp.moveaxis(pieces, 0, dim).reshape(dims)
+
+
+def doubled(x, axis):
+    size = lax.axis_size(axis)
+    blocks = x[None]
+    for level in range(size.bit_length() - 1):
+        bit = 1 << level
+        other = lax.ppermute(blocks, axis, [(i, i ^ bit) for i in range(size)])
+        both = jnp.stack([blocks, other])
+        upper = lax.axis_index(axis) >> level & 1
+        blocks = jnp.where(upper == 0, both, both[::-1]).reshape(-1, *x.shape)
+    return blocks
+
+
+def gather_by_bits(x, axis, dim):
+    return joined_along(doubled(x, axis), dim)
 
 
 def matmul(spec, left, right):
@@ -182,7 +204,7 @@
         (attn_query, attn_key, attn_value, attn_out, jnp.pad(columns, ((0, 0), (0, spare)))), axis=1
     )
     attn_all = lax.all_gather(packed, "shard", axis=0, tiled=True)
-    fc1_all = lax.all_gather(fc1_weight, "shard", axis=0, tiled=True)
+    fc1_all = gather_by_bits(fc1_weight, "shard", 0)
     fc2_all = lax.all_gather(fc2_weight, "shard", axis=0, tiled=True)
     small = attn_all[:, 4 * width : 4 * width + used]
     g1, b1, bq, bv, bo, g2, b2, bf2 = (small[:, i] for i in range(len(narrow)))

time: 431 us -> 517 us (1.20)
  waiting for transfers between devices: 320 us -> 391 us
  other arithmetic: 13.6 us -> 22.7 us
  starting transfers between devices: 0.46 us -> 5.75 us
    ppermute x0 -> x3, waiting for transfers between devices: none -> 207 us  [doubled(): other = lax.ppermute(blocks, axis, [(i, i ^ bit) for i in range(size)])]
    all_gather x1, waiting for transfers between devices: 54.1 us -> 0.01 us  [body(): attn_all = lax.all_gather(packed, 'shard', axis=0, tiled=True)]
    all_gather x1, waiting for transfers between devices: 45.7 us -> 0.01 us  [body(): fc2_all = lax.all_gather(fc2_weight, 'shard', axis=0, tiled=True)]
    all_gather x1 -> x0, waiting for transfers between devices: 36.8 us -> none  [body(): fc1_all = lax.all_gather(fc1_weight, 'shard', axis=0, tiled=True)]
    ppermute x0 -> x3, starting transfers between devices: none -> 5.32 us  [doubled(): other = lax.ppermute(blocks, axis, [(i, i ^ bit) for i in range(size)])]
  transfers between devices with their start and end apart: 7 -> 9, of which waited for: 7 -> 7; matrix products, arithmetic and copies ran while one was open for 16% -> 15% of each run, Pallas kernels for 0% -> 0%
where the time goes in v1:
time: 517 us; the launch traced here: 516 us
  waiting for transfers between devices  391 us (76%)
  matrix products  52.5 us (10%)
  local copies, waits for them, and re-layouts  29.1 us (6%)
  other arithmetic  22.7 us (4%)
  between operations  14.6 us (3%)
  starting transfers between devices  5.75 us (1%)
    ppermute x3, waiting for transfers between devices, doubled(): other = lax.ppermute(blocks, axis, [(i, i ^ bit) for i in range(size)])  207 us
    reduce_scatter x3, waiting for transfers between devices, owned(): lax.psum_scatter(grad.astype(bf16), 'shard', scatter_dimension=0, tiled=T...  124 us
    psum x1, waiting for transfers between devices, owned(): return lax.psum(part, 'replica').astype(f32)  60 us
    dot_general x18, matrix products, matmul(): return jnp.einsum(spec, left, right, preferred_element_type=jnp.float32)  52.5 us
  transfers between devices with their start and end apart: 9, of which 7 were waited for; matrix products, arithmetic and copies ran while one was open for 15% of the time, Pallas kernels for 0%

profile of v1, /device:TPU:0, one launch (start us, length us, event | category | flops | bytes accessed | tf_op | source)
XLA Modules:
  0.0 515.8 jit_solution(26501159931037581)
XLA Ops:
  9.1 0.9 constant_dynamic-update-slice_fusion.3
  10.0 0.9 constant_dynamic-update-slice_fusion.2
  10.9 0.9 constant_dynamic-update-slice_fusion.1
  11.8 0.9 constant_dynamic-update-slice_fusion
  14.3 1.8 collective-permute-done
  16.1 1.2 pad_maximum_fusion.2
  17.6 3.0 collective-permute-start.1
  20.7 65.8 %collective-permute-done.1 = bf16[2,96,3072]{2,1,0:T(8,128)(2,1)} collective-permute-done((bf16[2,96,3072]{2,1,0:T(8,128)(2,1)S(1)}, bf16[2,96,3072]{2,1,0:T(8,128)(2,1)}, u32[]{:S(2)}, u32[]{:S(2)}) %collective-permute-start.1) | collective-permute-done | bytes 1179680 | tf_op jit(solution)/shard_map/ppermute | solution.py:21
  86.5 1.5 pad_maximum_fusion.1
  88.7 1.8 collective-permute-start.2
  90.8 139.7 %collective-permute-done.2 = bf16[4,96,3072]{2,1,0:T(8,128)(2,1)} collective-permute-done((bf16[4,96,3072]{2,1,0:T(8,128)(2,1)S(1)}, bf16[4,96,3072]{2,1,0:T(8,128)(2,1)}, u32[]{:S(2)}, u32[]{:S(2)}) %collective-permute-start.2) | collective-permute-done | bytes 2359328 | tf_op jit(solution)/shard_map/ppermute | solution.py:21
  230.4 2.1 pad_maximum_fusion
  232.5 3.4 reverse_select_fusion
  235.9 1.0 slice_convert_fusion.1
  237.2 3.1 convert_reduce_fusion
  240.3 3.0 convolution_bitcast_fusion
  243.5 0.9 copy.96
  244.4 0.9 copy.97
  245.5 1.8 fusion.57
  248.5 1.9 fusion.58
  250.6 5.9 %multiply_convert_fusion.1 = (bf16[224,3072]{1,0:T(8,128)(2,1)}, f32[224,3072]{1,0:T(8,128)}) fusion(f32[3072]{0:T(1024)S(1)} %reshape.437, bf16[768,3072]{1,0:T(8,128)(2,1)} %bitcast.137, f32[1,224,768]{2,1,0:T(8,128)S(1)} %get-tuple-element.62, f32[768]{0:T(1024)S(1)} %get-tuple-element.18, f32[768]{0:T(1024)S(1)} %get-tuple-element.19, ...), kind=kOutput, calls=%fused_computation.22 | convolution fusion | flops 1061953536 | bytes 9555712 | tf_op jit(solution)/shard_map/cld,df->clf/dot_general | solution.py:33
  256.6 5.2 %fusion.59 = (bf16[3072]{0:T(1024)(128)(2,1)S(1)}, bf16[224,3072]{1,0:T(8,128)(2,1)S(1)}) fusion(f32[224,3072]{1,0:T(8,128)} %get-tuple-element.64, bf16[3072,768]{1,0:T(8,128)(2,1)} %all-gather.5.cloned.1.call-done, f32[1,224,768]{2,1,0:T(8,128)} %param.18), kind=kOutput, calls=%fused_computation.129 | convolution fusion | flops 1064702976 | bytes 9541632 | tf_op jit(solution)/shard_map/cld,fd->clf/dot_general | solution.py:33
  261.8 1.2 copy-done.14
  263.0 3.8 convolution_convert_fusion.2
  267.1 5.1 convolution_convert_fusion.1
  272.2 1.1 reshape.428
  273.3 4.6 fusion.21
  281.8 2.6 convolution_convert_fusion.6
  284.4 1.9 copy.99
  286.3 2.4 fusion.54
  288.7 1.1 stack.99
  289.8 1.9 multiply_reduce_fusion
  292.2 1.1 copy-done
  293.8 1.1 stack.98
  294.9 2.0 convolution_convert_fusion.4
  297.0 3.7 fusion.22
  303.4 2.3 concatenate.20
  306.2 2.6 convolution_convert_fusion
  308.9 2.6 fusion.1
  311.5 10.8 %reduce-scatter.6.cloned.1.call-done = bf16[96,3072]{1,0:T(8,128)(2,1)} async-done(((bf16[768,3072]{1,0:T(8,128)(2,1)}), bf16[96,3072]{1,0:T(8,128)(2,1)}) %reduce-scatter.6.cloned.1.call-update) | async-done | bytes 589840 | tf_op jit(solution)/shard_map/reduce_scatter | solution.py:220
  322.4 55.5 %reduce-scatter.8.cloned.1.call-done = bf16[384,768]{1,0:T(8,128)(2,1)} async-done(((bf16[3072,768]{1,0:T(8,128)(2,1)}), bf16[384,768]{1,0:T(8,128)(2,1)}) %reduce-scatter.8.cloned.1.call-update) | async-done | bytes 589840 | tf_op jit(solution)/shard_map/reduce_scatter | solution.py:220
  377.9 57.4 %reduce-scatter.4.cloned.1.call-done = bf16[96,3200]{1,0:T(8,128)(2,1)} async-done(((bf16[768,3200]{1,0:T(8,128)(2,1)}), bf16[96,3200]{1,0:T(8,128)(2,1)}) %reduce-scatter.4.cloned.1.call-update) | async-done | bytes 614416 | tf_op jit(solution)/shard_map/reduce_scatter | solution.py:220
  435.4 2.2 fusion.25
  437.6 4.4 fusion.13
  442.0 60.0 %all-reduce.5.cloned.1.call-done = (bf16[96,3200]{1,0:T(8,128)(2,1)}, bf16[96,3072]{1,0:T(8,128)(2,1)}, bf16[384,768]{1,0:T(8,128)(2,1)}) async-done(((bf16[96,3200]{1,0:T(8,128)(2,1)}, bf16[96,3072]{1,0:T(8,128)(2,1)}, bf16[384,768]{1,0:T(8,128)(2,1)}), (bf16[96,3200]{1,0:T(8,128)(2,1)}, bf16[96,3072]{1,0:T(8,128)(2,1)}, bf16[384,768]{1,0:T(8,128)(2,1)})) %all-reduce.5.cloned.1.call-update) | async-done | bytes 1794064 | tf_op jit(solution)/shard_map/psum | solution.py:221
  502.9 2.2 fusion.56
  505.9 1.1 convert_element_type.259
  507.0 1.1 convert_element_type.261
  (107 shorter events, 17.6 us)
Async XLA Ops:
  7.2 228.7 %all-gather.3.cloned.1.call-start = ((), (), s32[]{:S(2)}) async-start(), calls=%async_computation.3 | async-start | bytes 5529600 | tf_op jit(solution)/shard_map/all_gather | solution.py:206
  12.8 0.8 copy-start.15
  13.6 242.9 %all-gather.5.cloned.1.call-start = ((), (), s32[]{:S(2)}) async-start(), calls=%async_computation.4 | async-start | bytes 5308416 | tf_op jit(solution)/shard_map/all_gather | solution.py:208
  13.7 2.4 collective-permute-start
  17.6 68.9 %collective-permute-start.1 = (bf16[2,96,3072]{2,1,0:T(8,128)(2,1)S(1)}, bf16[2,96,3072]{2,1,0:T(8,128)(2,1)}, u32[]{:S(2)}, u32[]{:S(2)}) collective-permute-start(bf16[2,96,3072]{2,1,0:T(8,128)(2,1)S(1)} %get-tuple-element.49), channel_id=1, source_target_pairs={{0,2},{1,3},{2,0},{3,1},{4,6},{5,7},{6,4},{7,5},{8,10},{9,11},{10,... | collective-permute-start | bytes 3538952 | tf_op jit(solution)/shard_map/ppermute | solution.py:21
  20.7 301.7 %reduce-scatter.6.cloned.1.call-start = ((), (), s32[]{:S(2)}) async-start(), calls=%async_computation.6 | async-start | bytes 5308416 | tf_op jit(solution)/shard_map/reduce_scatter | solution.py:220
  88.1 2.4 copy-start.1
  88.7 141.8 %collective-permute-start.2 = (bf16[4,96,3072]{2,1,0:T(8,128)(2,1)S(1)}, bf16[4,96,3072]{2,1,0:T(8,128)(2,1)}, u32[]{:S(2)}, u32[]{:S(2)}) collective-permute-start(bf16[4,96,3072]{2,1,0:T(8,128)(2,1)S(1)} %bitcast.135), channel_id=1, source_target_pairs={{0,4},{1,5},{2,6},{3,7},{4,0},{5,1},{6,2},{7,3},{8,12},{9,13},{10,... | collective-permute-start | bytes 7077896 | tf_op jit(solution)/shard_map/ppermute | solution.py:21
  245.5 2.3 copy-start.7
  247.4 1.1 copy-start.2
  248.4 2.0 copy-start.9
  261.8 1.2 copy-start.14
  266.8 111.1 %reduce-scatter.8.cloned.1.call-start = ((), (), s32[]{:S(2)}) async-start(), calls=%async_computation.7 | async-start | bytes 5308416 | tf_op jit(solution)/shard_map/reduce_scatter | solution.py:220
  272.2 163.1 %reduce-scatter.4.cloned.1.call-start = ((), (), s32[]{:S(2)}) async-start(), calls=%async_computation.5 | async-start | bytes 5529600 | tf_op jit(solution)/shard_map/reduce_scatter | solution.py:220
  273.3 4.7 copy-start.13
  278.4 3.5 copy-start.4
  291.6 1.7 copy-start.8
  292.2 1.1 copy-start
  293.3 3.6 copy-start.3
  293.3 3.6 copy-start.24
  293.8 3.1 copy-start.25
  296.9 3.8 copy-start.26
  296.9 6.5 %copy-start.16 = (bf16[768,4]{1,0:T(8,128)(2,1)S(1)}, bf16[768,4]{1,0:T(8,128)(2,1)}, u32[]{:S(2)}) copy-start(bf16[768,4]{1,0:T(8,128)(2,1)} %reshape.428) | copy-start | bytes 18436
  296.9 6.4 %copy-start.17 = (bf16[768,1]{1,0:T(8,128)(2,1)S(1)}, bf16[768,1]{1,0:T(8,128)(2,1)}, u32[]{:S(2)}) copy-start(bf16[768,1]{1,0:T(8,128)(2,1)} %stack.100) | copy-start | bytes 4612
  297.0 6.4 %copy-start.18 = (bf16[768,1]{1,0:T(8,128)(2,1)S(1)}, bf16[768,1]{1,0:T(8,128)(2,1)}, u32[]{:S(2)}) copy-start(bf16[768,1]{1,0:T(8,128)(2,1)} %stack.102) | copy-start | bytes 4612
  297.0 6.4 %copy-start.19 = (bf16[768,1]{1,0:T(8,128)(2,1)S(1)}, bf16[768,1]{1,0:T(8,128)(2,1)}, u32[]{:S(2)}) copy-start(bf16[768,1]{1,0:T(8,128)(2,1)} %stack.101) | copy-start | bytes 4612
  297.0 6.4 %copy-start.20 = (bf16[768,1]{1,0:T(8,128)(2,1)S(1)}, bf16[768,1]{1,0:T(8,128)(2,1)}, u32[]{:S(2)}) copy-start(bf16[768,1]{1,0:T(8,128)(2,1)} %stack.103) | copy-start | bytes 4612
  300.7 0.8 copy-start.12
  300.7 5.0 copy-start.5
  300.7 5.0 copy-start.10
  306.2 2.6 copy-start.21
  311.5 126.1 %copy-start.11 = (bf16[224,3072]{1,0:T(8,128)(2,1)S(1)}, bf16[224,3072]{1,0:T(8,128)(2,1)}, u32[]{:S(2)}) copy-start(bf16[224,3072]{1,0:T(8,128)(2,1)} %get-tuple-element.63) | copy-start | bytes 4128772
  311.5 190.5 %all-reduce.5.cloned.1.call-start = ((), (), s32[]{:S(2)}) async-start(), calls=%async_computation.8 | async-start | bytes 3588096 | tf_op jit(solution)/shard_map/psum | solution.py:221
  502.0 3.1 copy-start.6
  502.0 3.9 copy-start.23
  502.9 4.1 copy-start.22
Sparse Core Ops, SparseCore 0:
  13.8 73.9 all-gather.2
  89.4 112.2 all-gather.4
  267.0 55.3 reduce-scatter.5
  324.5 53.3 reduce-scatter.7
  380.1 55.1 reduce-scatter.3
  438.7 63.2 all-reduce.4
